TPU v7x, 32 devices: a whole 2x2x4 slice. The times are simulated.
32 devices in a mesh: groups: 2 (over y), prow: 4 (over x, core), pcol: 4 (over z).
Axes of the slice: x: 2, y: 2, z: 4, core: 2. Of those that a mesh axis runs over, the one named last changes fastest.
Arguments:
- anc_inverse: float32 [4096, 2048], P(('groups', 'prow'), 'pcol'), parts along dimension 0
- anc_factor: float32 [8, 2048, 256], P('groups', ('prow', 'pcol')), parts along dimension 0, may hold values from -0.0625 to 0.0625
- win_factor: float32 [12, 256, 256], P('groups'), parts along dimension 0, may hold values from -0.1875 to 0.1875
- diag_inverse: float32 [8, 256, 256], P('groups'), parts along dimension 0
- first_reader: int32 [32], P('groups'), parts along dimension 0, may hold values from 0 to 4
Outputs:
- anc_panels: float32 [8, 2048, 256], P('groups', ('prow', 'pcol')), parts along dimension 0
- window_inverse: float32 [8, 4, 256, 256], P('groups'), parts along dimension 0
There are 2 independent parts, one for each index of `groups`. A program takes and returns all parts, laid end to end along the dimension named above; each array names one. Nothing has to cross between parts.
Inputs may be any that keep to these rules, and one draw needn't show every extreme that they name: Ancestor block b belongs to the pattern of supernode k exactly when first_reader[b] <= k; the value 4 puts it in no pattern, so patterns grow with k. Within each part, anc_inverse is symmetric: anc_inverse[r, s] = anc_inverse[s, r].
All inputs are finite; a program needn't handle non-finite values.
Results may differ from a plain program's by a relative error of at most 0.0003.
Values sent between devices are 32-bit elements; how exact they have to be, the bound alone decides.
A program may use at most 64 MiB of HBM per device.

v0:
```python
import jax
import jax.numpy as jnp
from jax import lax
from jax.sharding import PartitionSpec as P

BLK = 128


def broadcast(array, axis, root):
    mine = lax.axis_index(axis) == root
    return lax.psum(jnp.where(mine, array, jnp.zeros_like(array)), axis)


def to_columns(stacked, per_column, pcol_at):
    gathered = lax.all_gather(stacked, "pcol", axis=1, tiled=True)
    pieces = [
        broadcast(gathered, "prow", pcol_at * per_column + offset) for offset in range(per_column)
    ]
    return jnp.concatenate(pieces, axis=1)


def window_algebra(summed, upper_all, diag_inverse, window_count):
    highest = lax.Precision.HIGHEST
    blocks = [[None] * window_count for column in range(window_count)]
    for node in reversed(range(window_count)):
        linv = diag_inverse[node]
        later = list(range(node + 1, window_count))
        upper_u = upper_all[node]
        cross = {}
        for position, other in enumerate(later):
            term = summed[node][position]
            for second in later:
                term = term + jnp.dot(blocks[other][second], upper_u[second], precision=highest)
            cross[other] = term
        own = jnp.dot(linv.T, linv, precision=highest) + summed[node][len(later)]
        for other in later:
            own = own + jnp.dot(upper_u[other].T, cross[other], precision=highest)
        blocks[node][node] = own
        for other in later:
            blocks[other][node] = -cross[other]
            blocks[node][other] = -cross[other].T
    return jnp.stack([jnp.stack(blocks[row_at]) for row_at in range(window_count)])


def per_device(anc_inverse, anc_factor, win_factor, diag_inverse, first_reader):
    highest = lax.Precision.HIGHEST
    n_prow = lax.axis_size("prow")
    n_pcol = lax.axis_size("pcol")
    per_column = n_prow // n_pcol
    prow_at = lax.axis_index("prow")
    pcol_at = lax.axis_index("pcol")
    window_count = diag_inverse.shape[0]
    fine_rows = anc_factor.shape[1]
    start_row = (prow_at * n_pcol + pcol_at) * fine_rows
    block_of = (start_row + jnp.arange(fine_rows, dtype=jnp.int32)) // BLK
    block_ids = jnp.arange(first_reader.shape[0], dtype=jnp.int32)
    readers = jnp.sum(
        jnp.where(block_of[:, None] == block_ids[None, :], first_reader[None, :], 0), axis=1
    )
    row_masks = [(readers <= node).astype(jnp.float32)[:, None] for node in range(window_count)]
    lower_all = [
        jnp.dot(anc_factor[node], diag_inverse[node], precision=highest) * row_masks[node]
        for node in range(window_count)
    ]
    whole = to_columns(jnp.stack(lower_all), per_column, pcol_at)
    column_panels = [whole[node] for node in range(window_count)]
    panels = [None] * window_count
    upper_all = [None] * window_count
    summed = [None] * window_count
    for node in reversed(range(window_count)):
        linv = diag_inverse[node]
        later = list(range(node + 1, window_count))
        upper_u = {}
        for other in later:
            upper_u[other] = jnp.dot(
                win_factor[other * (other - 1) // 2 + node], linv, precision=highest
            )
        upper_all[node] = upper_u
        columns = column_panels[node]
        full_x = lax.psum_scatter(
            jnp.dot(anc_inverse, columns, precision=highest),
            "pcol",
            scatter_dimension=0,
            tiled=True,
        )
        for other in later:
            full_x = full_x + jnp.dot(panels[other], upper_u[other], precision=highest)
        partials = [jnp.dot(panels[other].T, lower_all[node], precision=highest) for other in later]
        partials.append(jnp.dot(lower_all[node].T, full_x, precision=highest))
        panels[node] = -full_x * row_masks[node]
        summed[node] = list(lax.psum(tuple(partials), ("prow", "pcol")))
    window_inverse = window_algebra(summed, upper_all, diag_inverse, window_count)
    return (jnp.stack(panels), window_inverse)


def solution(mesh):
    return jax.shard_map(
        per_device,
        mesh=mesh,
        in_specs=(
            P(("groups", "prow"), "pcol"),
            P("groups", ("prow", "pcol"), None),
            P("groups", None, None),
            P("groups", None, None),
            P("groups"),
        ),
        out_specs=(P("groups", ("prow", "pcol"), None), P("groups", None, None, None)),
        check_vma=False,
    )
```

profile of v0, /device:TPU:0, one launch (start us, length us, event | category | flops | bytes accessed | tf_op | source)
XLA Modules:
  0.0 358.3 jit_solution(12927005311065160913)
XLA Ops:
  8.1 1.3 convolution_multiply_fusion.3
  9.4 1.3 convolution_multiply_fusion.2
  10.8 1.3 convolution_multiply_fusion.1
  12.1 1.3 convolution_multiply_fusion
  14.4 48.7 %all-gather.2.cloned.1.call-done = f32[4,512,256]{2,1,0:T(8,128)} async-done(((f32[4,128,256]{2,1,0:T(8,128)}), f32[4,512,256]{2,1,0:T(8,128)}) %all-gather.2.cloned.1.call-update) | async-done | bytes 2097168 | tf_op jit(solution)/shard_map/all_gather | solution.py:15
  63.2 3.1 broadcast_select_fusion
  66.3 50.1 %all-reduce.4.cloned.1.call-done = f32[4,512,256]{2,1,0:T(8,128)} async-done(((f32[4,512,256]{2,1,0:T(8,128)}), f32[4,512,256]{2,1,0:T(8,128)}) %all-reduce.4.cloned.1.call-update) | async-done | bytes 2097168 | tf_op jit(solution)/shard_map/psum | solution.py:11
  116.4 2.8 convolution_bitcast_fusion
  119.4 2.9 convolution_bitcast_fusion.1
  122.4 1.3 fusion.5
  123.7 1.3 fusion.1
  125.0 2.9 convolution_bitcast_fusion.2
  128.0 1.3 fusion.3
  129.3 1.3 fusion.7
  130.7 1.3 fusion.9
  132.0 2.1 fusion.11
  134.1 2.9 convolution_bitcast_fusion.3
  137.2 4.0 %reduce-scatter.11.cloned.1.call-done = f32[128,256]{1,0:T(8,128)} async-done(((f32[512,256]{1,0:T(8,128)}), f32[128,256]{1,0:T(8,128)}) %reduce-scatter.11.cloned.1.call-update) | async-done | bytes 131088 | tf_op jit(solution)/shard_map/reduce_scatter | solution.py:80
  141.2 22.7 %reduce-scatter.9.cloned.1.call-done = f32[128,256]{1,0:T(8,128)} async-done(((f32[512,256]{1,0:T(8,128)}), f32[128,256]{1,0:T(8,128)}) %reduce-scatter.9.cloned.1.call-update) | async-done | bytes 131088 | tf_op jit(solution)/shard_map/reduce_scatter | solution.py:80
  163.9 1.4 convolution_add_fusion.29
  165.3 20.7 %reduce-scatter.7.cloned.1.call-done = f32[128,256]{1,0:T(8,128)} async-done(((f32[512,256]{1,0:T(8,128)}), f32[128,256]{1,0:T(8,128)}) %reduce-scatter.7.cloned.1.call-update) | async-done | bytes 131088 | tf_op jit(solution)/shard_map/reduce_scatter | solution.py:80
  186.0 1.3 convolution_add_fusion.28
  187.3 1.2 convolution_add_fusion.27
  188.5 2.2 fusion.80
  190.7 2.0 fusion.79
  192.7 2.1 fusion.66
  194.8 2.1 fusion.65
  196.8 1.2 fusion.63
  198.0 10.0 %reduce-scatter.5.cloned.1.call-done = f32[128,256]{1,0:T(8,128)} async-done(((f32[512,256]{1,0:T(8,128)}), f32[128,256]{1,0:T(8,128)}) %reduce-scatter.5.cloned.1.call-update) | async-done | bytes 131088 | tf_op jit(solution)/shard_map/reduce_scatter | solution.py:80
  208.1 1.3 convolution_add_fusion.26
  209.4 1.2 convolution_add_fusion.25
  211.0 2.1 fusion.78
  213.1 1.1 fusion.81
  214.2 1.2 fusion.76
  215.4 1.2 fusion.75
  216.6 1.2 fusion.74
  217.8 1.0 fusion.67
  218.9 1.1 multiply_bitcast_fusion
  220.8 99.6 %all-reduce.6.cloned.1.call-done = (f32[256,256]{1,0:T(8,128)}, f32[256,256]{1,0:T(8,128)}, f32[256,256]{0,1:T(8,128)}, f32[256,256]{1,0:T(8,128)}, f32[256,256]...) async-done(((f32[256,256]{1,0:T(8,128)}, f32[256,256]{1,0:T(8,128)}, ...) | async-done | bytes 2621456 | tf_op jit(solution)/shard_map/psum | solution.py:91
  320.3 1.5 convolution_add_fusion.20
  321.9 1.5 convolution_add_fusion.19
  323.4 1.5 convolution_add_fusion.14
  337.4 1.0 negate_bitcast_fusion.3
  339.9 1.3 fusion
  343.8 1.2 maximum_bitcast_fusion.2
  345.0 1.3 copy.48
  346.4 1.3 maximum_bitcast_fusion.3
  349.0 2.4 pad_maximum_fusion
  (123 shorter events, 21.0 us)
Async XLA Ops:
  7.2 109.3 %copy-start = (f32[512,512]{1,0:T(8,128)S(1)}, f32[512,512]{1,0:T(8,128)}, u32[]{:S(2)}) copy-start(f32[512,512]{1,0:T(8,128)} %param.5) | copy-start | bytes 3145732
  7.2 56.0 %all-gather.2.cloned.1.call-start = ((), (), s32[]{:S(2)}) async-start(), calls=%async_computation.4 | async-start | bytes 2621440 | tf_op jit(solution)/shard_map/all_gather | solution.py:15
  9.4 56.9 %copy-start.6 = (f32[128,256]{1,0:T(8,128)}, f32[128,256]{1,0:T(8,128)S(1)}, u32[]{:S(2)}) copy-start(f32[128,256]{1,0:T(8,128)S(1)} %convolution_multiply_fusion.3) | copy-start | bytes 393220
  10.7 55.5 %copy-start.13 = (f32[128,256]{1,0:T(8,128)}, f32[128,256]{1,0:T(8,128)S(1)}, u32[]{:S(2)}) copy-start(f32[128,256]{1,0:T(8,128)S(1)} %convolution_multiply_fusion.2) | copy-start | bytes 393220
  12.1 54.1 %copy-start.17 = (f32[128,256]{1,0:T(8,128)}, f32[128,256]{1,0:T(8,128)S(1)}, u32[]{:S(2)}) copy-start(f32[128,256]{1,0:T(8,128)S(1)} %convolution_multiply_fusion.1) | copy-start | bytes 393220
  13.5 52.8 %copy-start.19 = (f32[128,256]{1,0:T(8,128)}, f32[128,256]{1,0:T(8,128)S(1)}, u32[]{:S(2)}) copy-start(f32[128,256]{1,0:T(8,128)S(1)} %convolution_multiply_fusion) | copy-start | bytes 393220
  14.4 102.1 %all-reduce.4.cloned.1.call-start = ((), (), s32[]{:S(2)}) async-start(), calls=%async_computation.5 | async-start | bytes 4194304 | tf_op jit(solution)/shard_map/psum | solution.py:11
  66.3 74.9 %reduce-scatter.11.cloned.1.call-start = ((), (), s32[]{:S(2)}) async-start(), calls=%async_computation.9 | async-start | bytes 655360 | tf_op jit(solution)/shard_map/reduce_scatter | solution.py:80
  119.3 3.1 copy-start.1
  119.3 44.6 %reduce-scatter.9.cloned.1.call-start = ((), (), s32[]{:S(2)}) async-start(), calls=%async_computation.8 | async-start | bytes 655360 | tf_op jit(solution)/shard_map/reduce_scatter | solution.py:80
  122.3 63.7 %reduce-scatter.7.cloned.1.call-start = ((), (), s32[]{:S(2)}) async-start(), calls=%async_computation.7 | async-start | bytes 655360 | tf_op jit(solution)/shard_map/reduce_scatter | solution.py:80
  127.9 80.1 %reduce-scatter.5.cloned.1.call-start = ((), (), s32[]{:S(2)}) async-start(), calls=%async_computation.6 | async-start | bytes 655360 | tf_op jit(solution)/shard_map/reduce_scatter | solution.py:80
  137.0 183.4 %all-reduce.6.cloned.1.call-start = ((), (), s32[]{:S(2)}) async-start(), calls=%async_computation.10 | async-start | bytes 5242880 | tf_op jit(solution)/shard_map/psum | solution.py:91
  165.2 22.0 %copy-start.5 = (f32[128,256]{1,0:T(8,128)}, f32[128,256]{1,0:T(8,128)S(1)}, u32[]{:S(2)}) copy-start(f32[128,256]{1,0:T(8,128)S(1)} %convolution_add_fusion.29) | copy-start | bytes 393220
  186.0 6.7 %copy-start.14 = (f32[128,256]{1,0:T(8,128)S(1)}, f32[128,256]{1,0:T(8,128)}, u32[]{:S(2)}) copy-start(f32[128,256]{1,0:T(8,128)} %copy-done.13) | copy-start | bytes 393220
  186.0 8.8 %copy-start.7 = (f32[128,256]{1,0:T(8,128)S(1)}, f32[128,256]{1,0:T(8,128)}, u32[]{:S(2)}) copy-start(f32[128,256]{1,0:T(8,128)} %copy-done.6) | copy-start | bytes 393220
  188.5 8.4 %copy-start.16 = (f32[128,256]{1,0:T(8,128)}, f32[128,256]{1,0:T(8,128)S(1)}, u32[]{:S(2)}) copy-start(f32[128,256]{1,0:T(8,128)S(1)} %convolution_add_fusion.27) | copy-start | bytes 393220
  188.5 22.2 %copy-start.2 = (f32[128,256]{1,0:T(8,128)S(1)}, f32[128,256]{1,0:T(8,128)}, u32[]{:S(2)}) copy-start(f32[128,256]{1,0:T(8,128)} %reduce-scatter.11.cloned.1.call-done) | copy-start | bytes 393220
  208.1 5.0 %copy-start.20 = (f32[128,256]{1,0:T(8,128)S(1)}, f32[128,256]{1,0:T(8,128)}, u32[]{:S(2)}) copy-start(f32[128,256]{1,0:T(8,128)} %copy-done.19) | copy-start | bytes 393220
  208.1 6.1 %copy-start.18 = (f32[128,256]{1,0:T(8,128)S(1)}, f32[128,256]{1,0:T(8,128)}, u32[]{:S(2)}) copy-start(f32[128,256]{1,0:T(8,128)} %copy-done.17) | copy-start | bytes 393220
  208.1 7.3 %copy-start.15 = (f32[128,256]{1,0:T(8,128)S(1)}, f32[128,256]{1,0:T(8,128)}, u32[]{:S(2)}) copy-start(f32[128,256]{1,0:T(8,128)} %copy-done.13) | copy-start | bytes 393220
  208.1 8.5 %copy-start.8 = (f32[128,256]{1,0:T(8,128)S(1)}, f32[128,256]{1,0:T(8,128)}, u32[]{:S(2)}) copy-start(f32[128,256]{1,0:T(8,128)} %copy-done.6) | copy-start | bytes 393220
  211.0 5.6 %copy-start.21 = (f32[128,256]{1,0:T(8,128)}, f32[128,256]{1,0:T(8,128)S(1)}, u32[]{:S(2)}) copy-start(f32[128,256]{1,0:T(8,128)S(1)} %convolution_add_fusion.24) | copy-start | bytes 393220
  321.9 5.6 %copy-start.3 = (f32[256,256]{1,0:T(8,128)}, f32[256,256]{1,0:T(8,128)S(1)}, u32[]{:S(2)}) copy-start(f32[256,256]{1,0:T(8,128)S(1)} %convolution_add_fusion.20) | copy-start | bytes 786436
  321.9 4.5 %copy-start.36 = (f32[256,256]{1,0:T(8,128)S(1)}, f32[256,256]{1,0:T(8,128)}, u32[]{:S(2)}) copy-start(f32[256,256]{1,0:T(8,128)} %get-tuple-element.5) | copy-start | bytes 786436
  325.6 2.3 copy-start.32
  326.4 2.0 copy-start.9
  327.1 2.1 copy-start.35
  327.9 2.5 copy-start.34
  329.1 2.7 copy-start.11
  329.7 2.7 copy-start.31
  331.8 2.5 copy-start.33
  333.6 1.8 copy-start.30
  338.4 3.7 %copy-start.22 = (f32[1,256,256]{1,2,0:T(8,128)S(1)}, f32[1,256,256]{1,2,0:T(8,128)}, u32[]{:S(2)}) copy-start(f32[1,256,256]{1,2,0:T(8,128)} %get-tuple-element.21) | copy-start | bytes 786436
  339.0 4.8 %copy-start.12 = (f32[256,256]{0,1:T(8,128)S(1)}, f32[256,256]{0,1:T(8,128)}, u32[]{:S(2)}) copy-start(f32[256,256]{0,1:T(8,128)} %copy-done.11) | copy-start | bytes 786436
  343.8 2.6 copy-start.4
  345.0 2.7 copy-start.25
  346.3 1.4 copy-start.26
  346.4 1.4 copy-start.28
  346.4 1.4 copy-start.29
  346.4 1.5 copy-start.23
  346.4 1.5 copy-start.24
  346.4 1.6 copy-start.27
  347.7 1.3 copy-start.10
Sparse Core Ops, SparseCore 0:
  14.5 48.6 all-gather.1
  66.4 49.9 all-reduce.3
  119.4 21.7 reduce-scatter.10
  144.0 19.8 reduce-scatter.8
  166.1 19.8 reduce-scatter.6
  188.2 19.8 reduce-scatter.4
  217.9 102.3 all-reduce.5
where the time goes:
time: 359 us; the launch traced here: 358 us
  waiting for transfers between devices  256 us (71%)
  matrix products  65.6 us (18%)
  other arithmetic  16.4 us (5%)
  between operations  14.9 us (4%)
  local copies, waits for them, and re-layouts  5.02 us (1%)
    psum x1, waiting for transfers between devices, per_device(): summed[node] = list(lax.psum(tuple(partials), ('prow', 'pcol')))  99.6 us
    reduce_scatter x4, waiting for transfers between devices, per_device(): lax.psum_scatter(jnp.dot(anc_inverse, columns, precision=highest), 'pcol'...  57.4 us
    psum x1, waiting for transfers between devices, broadcast(): return lax.psum(jnp.where(mine, array, jnp.zeros_like(array)), axis)  50.1 us
    all_gather x1, waiting for transfers between devices, to_columns(): gathered = lax.all_gather(stacked, 'pcol', axis=1, tiled=True)  48.7 us
    dot_general x4, matrix products, per_device(): jnp.dot(anc_inverse, columns, precision=highest)  11.5 us
    dot_general x14, matrix products, window_algebra(): jnp.dot(blocks[other][second], upper_u[second], precision=highest)  9.39 us
    dot_general x6, matrix products, per_device(): jnp.dot(panels[other].T, lower_all[node], precision=highest)  8.88 us
    dot_general x6, matrix products, per_device(): jnp.dot(win_factor[other * (other - 1) // 2 + node], linv, precision=high...  8.71 us
  transfers between devices with their start and end apart: 7, of which 7 were waited for; matrix products, arithmetic and copies ran while one was open for 9% of the time, Pallas kernels for 0%

commit v1 on v0

--- a/solution.py
+++ b/solution.py
@@ -12,7 +12,29 @@
 
 
 def to_columns(stacked, per_column, pcol_at):
-    gathered = lax.all_gather(stacked, "pcol", axis=1, tiled=True)
+    oldest, item_now, current_block = (
+        jax.lax.axis_size("pcol"),
+        jax.lax.axis_index("pcol"),
+        stacked.shape[1],
+    )
+    parts_seen = tuple(((nth, (nth + 1) % oldest) for nth in range(oldest)))
+    tray = tuple(((nth, (nth - 1) % oldest) for nth in range(oldest)))
+    gathered = jnp.zeros(
+        (*stacked.shape[:1], oldest * current_block, *stacked.shape[2:]), stacked.dtype
+    )
+    gathered = lax.dynamic_update_slice_in_dim(gathered, stacked, item_now * current_block, axis=1)
+    aux = val = stacked
+    f_now = oldest // 2
+    for src_i in [*range(1, f_now + 1)]:
+        aux = jax.lax.ppermute(aux, "pcol", parts_seen)
+        gathered = lax.dynamic_update_slice_in_dim(
+            gathered, aux, (item_now - src_i) % oldest * current_block, axis=1
+        )
+        if src_i < oldest - f_now:
+            val = jax.lax.ppermute(val, "pcol", tray)
+            gathered = lax.dynamic_update_slice_in_dim(
+                gathered, val, (item_now + src_i) % oldest * current_block, axis=1
+            )
     pieces = [
         broadcast(gathered, "prow", pcol_at * per_column + offset) for offset in range(per_column)
     ]

time: 359 us -> 350 us (0.975)
  waiting for transfers between devices: 256 us -> 241 us
  starting transfers between devices: 0.47 us -> 5.48 us
    all_gather x1 -> x0, waiting for transfers between devices: 48.7 us -> none  [to_columns(): gathered = lax.all_gather(stacked, 'pcol', axis=1, tiled=True)]
    ppermute x0 -> x3, waiting for transfers between devices: none -> 32.5 us  [the longest x2 23.6 us: to_columns(): aux = jax.lax.ppermute(aux, 'pcol', parts_seen)]
    ppermute x0 -> x3, starting transfers between devices: none -> 5.05 us  [the longest x2 3.02 us: to_columns(): aux = jax.lax.ppermute(aux, 'pcol', parts_seen)]
  transfers between devices with their start and end apart: 7 -> 9, of which waited for: 7 -> 9; matrix products, arithmetic and copies ran while one was open for 9% -> 10% of each run, Pallas kernels for 0% -> 0%
where the time goes in v1:
time: 350 us; the launch traced here: 349 us
  waiting for transfers between devices  241 us (69%)
  matrix products  66.2 us (19%)
  between operations  14.9 us (4%)
  other arithmetic  13.6 us (4%)
  local copies, waits for them, and re-layouts  8.01 us (2%)
  starting transfers between devices  5.48 us (2%)
    psum x1, waiting for transfers between devices, per_device(): summed[node] = list(lax.psum(tuple(partials), ('prow', 'pcol')))  99.6 us
    reduce_scatter x4, waiting for transfers between devices, per_device(): lax.psum_scatter(jnp.dot(anc_inverse, columns, precision=highest), 'pcol'...  57.5 us
    psum x1, waiting for transfers between devices, broadcast(): return lax.psum(jnp.where(mine, array, jnp.zeros_like(array)), axis)  50.8 us
    ppermute x2, waiting for transfers between devices, to_columns(): aux = jax.lax.ppermute(aux, 'pcol', parts_seen)  23.6 us
    dot_general x4, matrix products, per_device(): jnp.dot(anc_inverse, columns, precision=highest)  11.5 us
    dot_general x14, matrix products, window_algebra(): jnp.dot(blocks[other][second], upper_u[second], precision=highest)  9.38 us
    ppermute x1, waiting for transfers between devices, to_columns(): val = jax.lax.ppermute(val, 'pcol', tray)  8.89 us
    dot_general x6, matrix products, per_device(): jnp.dot(panels[other].T, lower_all[node], precision=highest)  8.89 us
  transfers between devices with their start and end apart: 9, of which 9 were waited for; matrix products, arithmetic and copies ran while one was open for 10% of the time, Pallas kernels for 0%

profile of v1, /device:TPU:0, one launch (start us, length us, event | category | flops | bytes accessed | tf_op | source)
XLA Modules:
  0.0 348.7 jit_solution(6077640381998491846)
XLA Ops:
  8.1 1.3 convolution_multiply_fusion.3
  9.4 1.3 convolution_multiply_fusion.2
  10.8 1.3 convolution_multiply_fusion.1
  12.1 2.0 convolution_multiply_fusion
  15.9 3.0 collective-permute-start
  18.9 2.0 collective-permute-start.1
  21.0 13.1 %collective-permute-done = f32[4,128,256]{2,1,0:T(8,128)} collective-permute-done((f32[4,128,256]{2,1,0:T(8,128)}, f32[4,128,256]{2,1,0:T(8,128)}, u32[]{:S(2)}, u32[]{:S(2)}) %collective-permute-start) | collective-permute-done | bytes 524320 | tf_op jit(solution)/shard_map/ppermute | solution.py:29
  34.1 1.1 constant_dynamic-update-slice_fusion.1
  35.2 8.9 %collective-permute-done.1 = f32[4,128,256]{2,1,0:T(8,128)} collective-permute-done((f32[4,128,256]{2,1,0:T(8,128)}, f32[4,128,256]{2,1,0:T(8,128)}, u32[]{:S(2)}, u32[]{:S(2)}) %collective-permute-start.1) | collective-permute-done | bytes 524320 | tf_op jit(solution)/shard_map/ppermute | solution.py:34
  45.2 10.5 %collective-permute-done.2 = f32[4,128,256]{2,1,0:T(8,128)} collective-permute-done((f32[4,128,256]{2,1,0:T(8,128)}, f32[4,128,256]{2,1,0:T(8,128)}, u32[]{:S(2)}, u32[]{:S(2)}) %collective-permute-start.2) | collective-permute-done | bytes 524320 | tf_op jit(solution)/shard_map/ppermute | solution.py:29
  56.8 1.5 broadcast_select_fusion
  58.4 50.8 %all-reduce.4.cloned.1.call-done = f32[4,512,256]{2,1,0:T(8,128)} async-done(((f32[4,512,256]{2,1,0:T(8,128)}), f32[4,512,256]{2,1,0:T(8,128)}) %all-reduce.4.cloned.1.call-update) | async-done | bytes 2097168 | tf_op jit(solution)/shard_map/psum | solution.py:11
  109.2 2.8 convolution_bitcast_fusion
  112.1 2.9 convolution_bitcast_fusion.1
  115.2 1.3 fusion.5
  116.5 1.3 fusion.1
  117.8 2.9 convolution_bitcast_fusion.2
  120.8 1.3 fusion.3
  122.1 1.3 fusion.7
  123.5 1.3 fusion.9
  124.8 2.0 fusion.11
  126.8 2.9 convolution_bitcast_fusion.3
  130.0 4.0 %reduce-scatter.11.cloned.1.call-done = f32[128,256]{1,0:T(8,128)} async-done(((f32[512,256]{1,0:T(8,128)}), f32[128,256]{1,0:T(8,128)}) %reduce-scatter.11.cloned.1.call-update) | async-done | bytes 131088 | tf_op jit(solution)/shard_map/reduce_scatter | solution.py:102
  134.0 22.8 %reduce-scatter.9.cloned.1.call-done = f32[128,256]{1,0:T(8,128)} async-done(((f32[512,256]{1,0:T(8,128)}), f32[128,256]{1,0:T(8,128)}) %reduce-scatter.9.cloned.1.call-update) | async-done | bytes 131088 | tf_op jit(solution)/shard_map/reduce_scatter | solution.py:102
  156.7 1.4 convolution_add_fusion.29
  158.1 20.8 %reduce-scatter.7.cloned.1.call-done = f32[128,256]{1,0:T(8,128)} async-done(((f32[512,256]{1,0:T(8,128)}), f32[128,256]{1,0:T(8,128)}) %reduce-scatter.7.cloned.1.call-update) | async-done | bytes 131088 | tf_op jit(solution)/shard_map/reduce_scatter | solution.py:102
  178.9 1.3 convolution_add_fusion.28
  180.1 1.2 convolution_add_fusion.27
  181.4 2.2 fusion.80
  183.6 2.0 fusion.79
  185.6 2.1 fusion.66
  187.7 2.1 fusion.65
  189.7 1.2 fusion.63
  190.9 9.9 %reduce-scatter.5.cloned.1.call-done = f32[128,256]{1,0:T(8,128)} async-done(((f32[512,256]{1,0:T(8,128)}), f32[128,256]{1,0:T(8,128)}) %reduce-scatter.5.cloned.1.call-update) | async-done | bytes 131088 | tf_op jit(solution)/shard_map/reduce_scatter | solution.py:102
  200.9 1.3 convolution_add_fusion.26
  202.2 1.2 convolution_add_fusion.25
  203.8 2.1 fusion.78
  205.9 1.1 fusion.81
  207.0 1.2 fusion.76
  208.2 1.2 fusion.75
  209.4 1.2 fusion.74
  213.6 99.6 %all-reduce.6.cloned.1.call-done = (f32[256,256]{1,0:T(8,128)}, f32[256,256]{1,0:T(8,128)}, f32[256,256]{0,1:T(8,128)}, f32[256,256]{1,0:T(8,128)}, f32[256,256]...) async-done(((f32[256,256]{1,0:T(8,128)}, f32[256,256]{1,0:T(8,128)}, ...) | async-done | bytes 2621456 | tf_op jit(solution)/shard_map/psum | solution.py:113
  313.2 1.5 convolution_add_fusion.20
  314.8 1.5 convolution_add_fusion.19
  316.3 1.5 convolution_add_fusion.14
  333.0 1.3 fusion
  337.8 1.3 maximum_bitcast_fusion.3
  339.4 2.4 pad_maximum_fusion
  (132 shorter events, 27.1 us)
Async XLA Ops:
  7.2 102.1 %copy-start = (f32[512,512]{1,0:T(8,128)S(1)}, f32[512,512]{1,0:T(8,128)}, u32[]{:S(2)}) copy-start(f32[512,512]{1,0:T(8,128)} %param.5) | copy-start | bytes 3145732
  7.2 102.0 %all-reduce.4.cloned.1.call-start = ((), (), s32[]{:S(2)}) async-start(), calls=%async_computation.4 | async-start | bytes 4194304 | tf_op jit(solution)/shard_map/psum | solution.py:11
  9.4 48.9 %copy-start.6 = (f32[128,256]{1,0:T(8,128)}, f32[128,256]{1,0:T(8,128)S(1)}, u32[]{:S(2)}) copy-start(f32[128,256]{1,0:T(8,128)S(1)} %convolution_multiply_fusion.3) | copy-start | bytes 393220
  10.7 47.6 %copy-start.12 = (f32[128,256]{1,0:T(8,128)}, f32[128,256]{1,0:T(8,128)S(1)}, u32[]{:S(2)}) copy-start(f32[128,256]{1,0:T(8,128)S(1)} %convolution_multiply_fusion.2) | copy-start | bytes 393220
  12.1 3.8 %copy-start.18 = (f32[128,256]{1,0:T(8,128)}, f32[128,256]{1,0:T(8,128)S(1)}, u32[]{:S(2)}) copy-start(f32[128,256]{1,0:T(8,128)S(1)} %convolution_multiply_fusion.1) | copy-start | bytes 393220
  14.1 0.9 copy-start.20
  15.9 18.2 %collective-permute-start = (f32[4,128,256]{2,1,0:T(8,128)}, f32[4,128,256]{2,1,0:T(8,128)}, u32[]{:S(2)}, u32[]{:S(2)}) collective-permute-start(f32[4,128,256]{2,1,0:T(8,128)} %get-tuple-element.12), channel_id=1, source_target_pairs={{0,1},{1,2},{2,3},{3,0},{4,5},{5,6},{6,7},{7,4},{8,9},{9,10},{10,1... | collective-permute-start | bytes 1572872 | tf_op jit(solution)/shard_map/ppermute | solution.py:29
  18.9 25.2 %collective-permute-start.1 = (f32[4,128,256]{2,1,0:T(8,128)}, f32[4,128,256]{2,1,0:T(8,128)}, u32[]{:S(2)}, u32[]{:S(2)}) collective-permute-start(f32[4,128,256]{2,1,0:T(8,128)} %get-tuple-element.12), channel_id=1, source_target_pairs={{0,3},{1,0},{2,1},{3,2},{4,7},{5,4},{6,5},{7,6},{8,11},{9,8},{10,9... | collective-permute-start | bytes 1572872 | tf_op jit(solution)/shard_map/ppermute | solution.py:34
  34.1 21.6 %collective-permute-start.2 = (f32[4,128,256]{2,1,0:T(8,128)}, f32[4,128,256]{2,1,0:T(8,128)}, u32[]{:S(2)}, u32[]{:S(2)}) collective-permute-start(f32[4,128,256]{2,1,0:T(8,128)} %collective-permute-done), channel_id=1, source_target_pairs={{0,1},{1,2},{2,3},{3,0},{4,5},{5,6},{6,7},{7,4},{8,9},{9,10},{10,1... | collective-permute-start | bytes 1572872 | tf_op jit(solution)/shard_map/ppermute | solution.py:29
  58.4 75.6 %reduce-scatter.11.cloned.1.call-start = ((), (), s32[]{:S(2)}) async-start(), calls=%async_computation.8 | async-start | bytes 655360 | tf_op jit(solution)/shard_map/reduce_scatter | solution.py:102
  112.1 3.1 copy-start.1
  112.1 44.6 %reduce-scatter.9.cloned.1.call-start = ((), (), s32[]{:S(2)}) async-start(), calls=%async_computation.7 | async-start | bytes 655360 | tf_op jit(solution)/shard_map/reduce_scatter | solution.py:102
  115.1 63.8 %reduce-scatter.7.cloned.1.call-start = ((), (), s32[]{:S(2)}) async-start(), calls=%async_computation.6 | async-start | bytes 655360 | tf_op jit(solution)/shard_map/reduce_scatter | solution.py:102
  120.7 80.2 %reduce-scatter.5.cloned.1.call-start = ((), (), s32[]{:S(2)}) async-start(), calls=%async_computation.5 | async-start | bytes 655360 | tf_op jit(solution)/shard_map/reduce_scatter | solution.py:102
  129.7 183.5 %all-reduce.6.cloned.1.call-start = ((), (), s32[]{:S(2)}) async-start(), calls=%async_computation.9 | async-start | bytes 5242880 | tf_op jit(solution)/shard_map/psum | solution.py:113
  158.1 22.0 %copy-start.5 = (f32[128,256]{1,0:T(8,128)}, f32[128,256]{1,0:T(8,128)S(1)}, u32[]{:S(2)}) copy-start(f32[128,256]{1,0:T(8,128)S(1)} %convolution_add_fusion.29) | copy-start | bytes 393220
  178.9 6.7 %copy-start.13 = (f32[128,256]{1,0:T(8,128)S(1)}, f32[128,256]{1,0:T(8,128)}, u32[]{:S(2)}) copy-start(f32[128,256]{1,0:T(8,128)} %copy-done.12) | copy-start | bytes 393220
  178.9 8.8 %copy-start.7 = (f32[128,256]{1,0:T(8,128)S(1)}, f32[128,256]{1,0:T(8,128)}, u32[]{:S(2)}) copy-start(f32[128,256]{1,0:T(8,128)} %copy-done.6) | copy-start | bytes 393220
  181.4 8.4 %copy-start.15 = (f32[128,256]{1,0:T(8,128)}, f32[128,256]{1,0:T(8,128)S(1)}, u32[]{:S(2)}) copy-start(f32[128,256]{1,0:T(8,128)S(1)} %convolution_add_fusion.27) | copy-start | bytes 393220
  181.4 22.1 %copy-start.2 = (f32[128,256]{1,0:T(8,128)S(1)}, f32[128,256]{1,0:T(8,128)}, u32[]{:S(2)}) copy-start(f32[128,256]{1,0:T(8,128)} %reduce-scatter.11.cloned.1.call-done) | copy-start | bytes 393220
  200.9 5.0 %copy-start.21 = (f32[128,256]{1,0:T(8,128)S(1)}, f32[128,256]{1,0:T(8,128)}, u32[]{:S(2)}) copy-start(f32[128,256]{1,0:T(8,128)} %convolution_multiply_fusion) | copy-start | bytes 393220
  200.9 6.1 %copy-start.19 = (f32[128,256]{1,0:T(8,128)S(1)}, f32[128,256]{1,0:T(8,128)}, u32[]{:S(2)}) copy-start(f32[128,256]{1,0:T(8,128)} %copy-done.18) | copy-start | bytes 393220
  200.9 7.3 %copy-start.14 = (f32[128,256]{1,0:T(8,128)S(1)}, f32[128,256]{1,0:T(8,128)}, u32[]{:S(2)}) copy-start(f32[128,256]{1,0:T(8,128)} %copy-done.12) | copy-start | bytes 393220
  200.9 8.5 %copy-start.8 = (f32[128,256]{1,0:T(8,128)S(1)}, f32[128,256]{1,0:T(8,128)}, u32[]{:S(2)}) copy-start(f32[128,256]{1,0:T(8,128)} %copy-done.6) | copy-start | bytes 393220
  203.8 5.6 %copy-start.22 = (f32[128,256]{1,0:T(8,128)}, f32[128,256]{1,0:T(8,128)S(1)}, u32[]{:S(2)}) copy-start(f32[128,256]{1,0:T(8,128)S(1)} %convolution_add_fusion.24) | copy-start | bytes 393220
  314.7 5.6 %copy-start.3 = (f32[256,256]{1,0:T(8,128)}, f32[256,256]{1,0:T(8,128)S(1)}, u32[]{:S(2)}) copy-start(f32[256,256]{1,0:T(8,128)S(1)} %convolution_add_fusion.20) | copy-start | bytes 786436
  314.8 4.6 %copy-start.37 = (f32[256,256]{1,0:T(8,128)S(1)}, f32[256,256]{1,0:T(8,128)}, u32[]{:S(2)}) copy-start(f32[256,256]{1,0:T(8,128)} %get-tuple-element.5) | copy-start | bytes 786436
  318.5 2.3 copy-start.33
  319.3 2.0 copy-start.9
  319.9 2.1 copy-start.36
  320.7 2.5 copy-start.35
  322.0 2.7 copy-start.10
  322.6 2.7 copy-start.32
  324.6 2.5 copy-start.34
  326.5 2.1 copy-start.31
  327.1 0.7 copy-start.16
  331.5 3.7 %copy-start.23 = (f32[1,256,256]{1,2,0:T(8,128)S(1)}, f32[1,256,256]{1,2,0:T(8,128)}, u32[]{:S(2)}) copy-start(f32[1,256,256]{1,2,0:T(8,128)} %get-tuple-element.23) | copy-start | bytes 786436
  332.1 4.8 %copy-start.11 = (f32[256,256]{0,1:T(8,128)S(1)}, f32[256,256]{0,1:T(8,128)}, u32[]{:S(2)}) copy-start(f32[256,256]{0,1:T(8,128)} %copy-done.10) | copy-start | bytes 786436
  336.8 1.0 copy-start.4
  337.3 1.8 copy-start.26
  337.3 1.8 copy-start.27
  337.3 1.8 copy-start.29
  337.3 1.8 copy-start.30
  337.8 1.4 copy-start.17
  337.8 1.4 copy-start.24
  337.8 1.4 copy-start.25
  337.8 1.5 copy-start.28
Sparse Core Ops, SparseCore 0:
  58.5 50.7 all-reduce.3
  112.2 21.7 reduce-scatter.10
  136.9 19.7 reduce-scatter.8
  159.0 19.8 reduce-scatter.6
  181.1 19.7 reduce-scatter.4
  210.7 102.4 all-reduce.5
